TPU v7x, 32 devices: a whole 2x2x4 slice. The times are simulated.
32 devices in a mesh: seq: 16 (over z, y, core), head: 2 (over x).
Axes of the slice: x: 2, y: 2, z: 4, core: 2. Of those that a mesh axis runs over, the one named last changes fastest.
Arguments:
- queries: bfloat16 [4, 64, 64, 128], P(None, None, 'head'), may hold values from -15 to 15
- new_keys: bfloat16 [4, 64, 8, 128], P(None, None, 'head'), may hold values from -16 to 16
- new_values: bfloat16 [4, 64, 8, 128], P(None, None, 'head'), may hold values from -6 to 6
- cache_keys: bfloat16 [4, 32768, 8, 128], P(None, 'seq', 'head'), may hold values from -6 to 6
- cache_values: bfloat16 [4, 32768, 8, 128], P(None, 'seq', 'head'), may hold values from -6 to 6
- parents: int32 [4, 64], replicated, may hold values from 0 to 63, as said below
- kv_lengths: int32 [4], replicated, may hold values from 1 to 32768
- out_weight: bfloat16 [8192, 8192], P('head', 'seq'), may hold values from -0.5 to 0.5
Outputs:
- mixed: bfloat16 [256, 8192], P('head', 'seq')
Inputs may be any that keep to these rules, and one draw needn't show every extreme that they name: parents[r, 0] = 0 for the root; for i >= 1, parents[r, i] < i.
All inputs are finite; a program needn't handle non-finite values.
Results may differ from a plain program's by a relative error of at most 0.0045.
Values may be sent and summed in bfloat16 or wider, within the bound.
A program may use at most 128 MiB of HBM per device.

v0:
```python
import math

import jax
import jax.numpy as jnp
from jax import lax
from jax.sharding import PartitionSpec as P

lowest = -1e30


def ancestors(parent_row):
    tree_size = parent_row.shape[0]
    indices = jnp.arange(tree_size, dtype=jnp.int32)
    parent_link = (parent_row[:, None] == indices[None, :]).astype(jnp.float32)
    itself = (indices[:, None] == indices[None, :]).astype(jnp.float32)
    reached = jnp.maximum(parent_link, itself)
    for repeat in range(max(1, (tree_size - 1).bit_length())):
        reached = jnp.minimum(jnp.dot(reached, reached, precision=lax.Precision.HIGHEST), 1.0)
    return reached


def partial_scores(query_rows, keys, values, allowed, score_scale):
    scores = (
        jnp.einsum("kqd,pkd->kqp", query_rows, keys, preferred_element_type=jnp.float32)
        * score_scale
    )
    scores = jnp.where(allowed, scores, lowest)
    maxima = jnp.max(scores, axis=-1)
    weights = jnp.where(allowed, jnp.exp(scores - maxima[..., None]), 0.0)
    totals = jnp.sum(weights, axis=-1)
    weighted = jnp.einsum(
        "kqp,pkd->kqd", weights.astype(jnp.bfloat16), values, preferred_element_type=jnp.float32
    )
    return (maxima, totals, weighted)


def body(queries, new_keys, new_values, cache_keys, cache_values, parents, kv_lengths, out_weight):
    requests, tree_size, heads, head_size = queries.shape
    kv_heads = new_keys.shape[2]
    group_size = heads // kv_heads
    block_size = cache_keys.shape[1]
    score_scale = 1.0 / math.sqrt(head_size)
    tokens = requests * tree_size
    positions = lax.axis_index("seq") * block_size + jnp.arange(block_size, dtype=jnp.int32)

    def token_order(maxima, totals, weighted):
        maxima = (
            maxima.reshape(kv_heads, tree_size, group_size)
            .transpose(1, 0, 2)
            .reshape(tree_size, heads)
        )
        totals = (
            totals.reshape(kv_heads, tree_size, group_size)
            .transpose(1, 0, 2)
            .reshape(tree_size, heads)
        )
        weighted = weighted.reshape(kv_heads, tree_size, group_size, head_size).transpose(
            1, 0, 2, 3
        )
        return (maxima, totals, weighted.reshape(tree_size, heads, head_size))

    def one_request(request_items):
        query, tree_keys, tree_values, past_keys, past_values, parent_row, length = request_items
        query_rows = query.reshape(tree_size, kv_heads, group_size, head_size).transpose(1, 0, 2, 3)
        query_rows = query_rows.reshape(kv_heads, tree_size * group_size, head_size)
        cache_max, cache_tot, cache_acc = partial_scores(
            query_rows, past_keys, past_values, positions < length, score_scale
        )
        tree_allowed = jnp.repeat(ancestors(parent_row), group_size, axis=0) > 0.5
        tree_max, tree_tot, tree_acc = partial_scores(
            query_rows, tree_keys, tree_values, tree_allowed, score_scale
        )
        return (
            token_order(cache_max, cache_tot, cache_acc),
            token_order(tree_max, tree_tot, tree_acc),
        )

    cache_part, tree_part = lax.map(
        one_request, (queries, new_keys, new_values, cache_keys, cache_values, parents, kv_lengths)
    )
    cache_max = cache_part[0].reshape(tokens, heads)
    cache_tot = cache_part[1].reshape(tokens, heads)
    cache_acc = cache_part[2].reshape(tokens, heads, head_size)
    tree_max = tree_part[0].reshape(tokens, heads)
    tree_tot = tree_part[1].reshape(tokens, heads)
    tree_acc = tree_part[2].reshape(tokens, heads, head_size)
    overall = lax.pmax(cache_max, "seq")
    overall = jnp.maximum(overall, tree_max)
    factor = jnp.exp(cache_max - overall)
    shared_acc, shared_tot = (
        lax.psum_scatter(cache_acc * factor[..., None], "seq", scatter_dimension=0, tiled=True),
        lax.psum_scatter(cache_tot * factor, "seq", scatter_dimension=0, tiled=True),
    )
    row_count = tokens // lax.axis_size("seq")
    first_row = lax.axis_index("seq") * row_count

    def take_rows(array):
        return lax.dynamic_slice_in_dim(array, first_row, row_count, 0)

    tree_factor = jnp.exp(take_rows(tree_max) - take_rows(overall))
    weighted = shared_acc + take_rows(tree_acc) * tree_factor[..., None]
    totals = shared_tot + take_rows(tree_tot) * tree_factor
    share = (
        (weighted / totals[..., None]).astype(jnp.bfloat16).reshape(row_count, heads * head_size)
    )
    attended = lax.all_gather(share, "seq", axis=0, tiled=True)
    mixed = lax.psum_scatter(
        jnp.dot(attended, out_weight, preferred_element_type=jnp.float32),
        "head",
        scatter_dimension=0,
        tiled=True,
    )
    return mixed.astype(jnp.bfloat16)


def solution(mesh):
    placed = (
        P(None, None, "head", None),
        P(None, None, "head", None),
        P(None, None, "head", None),
        P(None, "seq", "head", None),
        P(None, "seq", "head", None),
        P(),
        P(),
        P("head", "seq"),
    )
    return jax.shard_map(
        body, mesh=mesh, in_specs=placed, out_specs=P("head", "seq"), check_vma=False
    )
```

profile of v0, /device:TPU:0, one launch (start us, length us, event | category | flops | bytes accessed | tf_op | source)
XLA Modules:
  0.0 414.5 jit_solution(2779970047454667348)
XLA Ops:
  6.5 145.8 %while.21 = (s32[]{:T(128)}, f32[4,64,32]{1,0,2:T(4,128)S(1)}, f32[4,64,32]{1,0,2:T(4,128)S(1)}, f32[4,64,32,128]{3,2,1,0:T(8,128)}, f32[4,64,32]{1,0,2:T(4,128)...) while((s32[]{:T(128)}, f32[4,64,32]{1,0,2:T(4,128)S(1)}, ...), condition=%wide.region_5.6_spmd.clone, body=%wide.region_0.5_spmd.clone.sunk | while | flops 2289217536 | bytes 81249280 | solution.py:78
  6.6 1.5 dynamic_slice.82
  8.0 0.7 add_compare_fusion.2
  8.7 2.0 constant_dynamic-slice_fusion.9
  10.7 7.2 %fusion.81 = (f32[4,512]{1,0:T(4,128)S(1)}, f32[4,512,2048]{2,1,0:T(8,128)}) fusion(pred[2048]{0:T(1024)(128)(4,1)S(1)} %add_compare_fusion.2, bf16[1,2048,4,128]{3,2,1,0:T(4,128)(2,1)S(1)} %constant_dynamic-slice_fusion.9, bf16[4,64,32,128]{3,2,1,0:T(8,128)(2,1)S(1)} %copy-done, s32[]{:T(128)S(6)} %copy.150), kind=kOutput, calls=%fused_computation.3.clone.1 | convolution fusion | flops 1086322688 | bytes 19408900 | tf_op jit(solution)/shard_map/while/body/eval_jaxpr/kqd,pkd->kqp/dot_general | solution.py:24
  18.2 8.1 %fusion.82 = f32[4,512]{1,0:T(4,128)S(1)} fusion(f32[4,512,2048]{2,1,0:T(8,128)} %get-tuple-element.325, f32[4,512]{1,0:T(4,128)S(1)} %get-tuple-element.324, pred[2048]{0:T(1024)(128)(4,1)S(1)} %add_compare_fusion.2), kind=kLoop, calls=%fused_computation.5.clone.1 | loop fusion | flops 20969472 | bytes 16795648 | tf_op jit(solution)/shard_map/while/body/eval_jaxpr/reduce_sum | solution.py:30
  26.6 0.9 constant_dynamic-slice_fusion.10
  27.5 0.7 fusion.83
  29.4 0.3 fusion.85
  29.8 0.9 constant_dynamic-slice_fusion.11
  30.6 0.4 convolution_bitcast_fusion.2
  31.0 2.0 constant_dynamic-slice_fusion.12
  33.0 7.7 %fusion.86 = f32[64,4,8,128]{3,2,0,1:T(8,128)S(1)} fusion(bf16[1,2048,4,128]{3,2,1,0:T(4,128)(2,1)S(1)} %constant_dynamic-slice_fusion.12, f32[4,512,2048]{2,1,0:T(8,128)} %get-tuple-element.325, f32[4,512]{1,0:T(4,128)S(1)} %get-tuple-element.324, pred[2048]{0:T(1024)(128)(4,1)S(1)} %add_compare_fusion.2), kind=kOutput, calls=%fused_computation.11.clone.1 | convolution fusion | flops 1094713344 | bytes 19933184 | tf_op jit(solution)/shard_map/while/body/eval_jaxpr/kqp,pkd->kqd/dot_general | solution.py:31
  40.7 1.6 bitcast_dynamic-update-slice_fusion.3
  43.0 1.5 dynamic_slice.82
  44.5 0.7 add_compare_fusion.2
  45.2 2.0 constant_dynamic-slice_fusion.9
  47.2 7.2 %fusion.81 = (f32[4,512]{1,0:T(4,128)S(1)}, f32[4,512,2048]{2,1,0:T(8,128)}) fusion(pred[2048]{0:T(1024)(128)(4,1)S(1)} %add_compare_fusion.2, bf16[1,2048,4,128]{3,2,1,0:T(4,128)(2,1)S(1)} %constant_dynamic-slice_fusion.9, bf16[4,64,32,128]{3,2,1,0:T(8,128)(2,1)S(1)} %copy-done, s32[]{:T(128)S(6)} %copy.150), kind=kOutput, calls=%fused_computation.3.clone.1 | convolution fusion | flops 1086322688 | bytes 19408900 | tf_op jit(solution)/shard_map/while/body/eval_jaxpr/kqd,pkd->kqp/dot_general | solution.py:24
  54.7 8.1 %fusion.82 = f32[4,512]{1,0:T(4,128)S(1)} fusion(f32[4,512,2048]{2,1,0:T(8,128)} %get-tuple-element.325, f32[4,512]{1,0:T(4,128)S(1)} %get-tuple-element.324, pred[2048]{0:T(1024)(128)(4,1)S(1)} %add_compare_fusion.2), kind=kLoop, calls=%fused_computation.5.clone.1 | loop fusion | flops 20969472 | bytes 16795648 | tf_op jit(solution)/shard_map/while/body/eval_jaxpr/reduce_sum | solution.py:30
  63.1 0.9 constant_dynamic-slice_fusion.10
  63.9 0.7 fusion.83
  65.9 0.3 fusion.85
  66.2 0.9 constant_dynamic-slice_fusion.11
  67.1 0.4 convolution_bitcast_fusion.2
  67.5 2.0 constant_dynamic-slice_fusion.12
  69.5 7.7 %fusion.86 = f32[64,4,8,128]{3,2,0,1:T(8,128)S(1)} fusion(bf16[1,2048,4,128]{3,2,1,0:T(4,128)(2,1)S(1)} %constant_dynamic-slice_fusion.12, f32[4,512,2048]{2,1,0:T(8,128)} %get-tuple-element.325, f32[4,512]{1,0:T(4,128)S(1)} %get-tuple-element.324, pred[2048]{0:T(1024)(128)(4,1)S(1)} %add_compare_fusion.2), kind=kOutput, calls=%fused_computation.11.clone.1 | convolution fusion | flops 1094713344 | bytes 19933184 | tf_op jit(solution)/shard_map/while/body/eval_jaxpr/kqp,pkd->kqd/dot_general | solution.py:31
  77.1 1.6 bitcast_dynamic-update-slice_fusion.3
  79.5 1.5 dynamic_slice.82
  81.0 0.7 add_compare_fusion.2
  81.7 2.0 constant_dynamic-slice_fusion.9
  83.7 7.2 %fusion.81 = (f32[4,512]{1,0:T(4,128)S(1)}, f32[4,512,2048]{2,1,0:T(8,128)}) fusion(pred[2048]{0:T(1024)(128)(4,1)S(1)} %add_compare_fusion.2, bf16[1,2048,4,128]{3,2,1,0:T(4,128)(2,1)S(1)} %constant_dynamic-slice_fusion.9, bf16[4,64,32,128]{3,2,1,0:T(8,128)(2,1)S(1)} %copy-done, s32[]{:T(128)S(6)} %copy.150), kind=kOutput, calls=%fused_computation.3.clone.1 | convolution fusion | flops 1086322688 | bytes 19408900 | tf_op jit(solution)/shard_map/while/body/eval_jaxpr/kqd,pkd->kqp/dot_general | solution.py:24
  91.2 8.1 %fusion.82 = f32[4,512]{1,0:T(4,128)S(1)} fusion(f32[4,512,2048]{2,1,0:T(8,128)} %get-tuple-element.325, f32[4,512]{1,0:T(4,128)S(1)} %get-tuple-element.324, pred[2048]{0:T(1024)(128)(4,1)S(1)} %add_compare_fusion.2), kind=kLoop, calls=%fused_computation.5.clone.1 | loop fusion | flops 20969472 | bytes 16795648 | tf_op jit(solution)/shard_map/while/body/eval_jaxpr/reduce_sum | solution.py:30
  99.5 0.9 constant_dynamic-slice_fusion.10
  100.4 0.7 fusion.83
  102.4 0.3 fusion.85
  102.7 0.9 constant_dynamic-slice_fusion.11
  103.6 0.4 convolution_bitcast_fusion.2
  104.0 2.0 constant_dynamic-slice_fusion.12
  105.9 7.7 %fusion.86 = f32[64,4,8,128]{3,2,0,1:T(8,128)S(1)} fusion(bf16[1,2048,4,128]{3,2,1,0:T(4,128)(2,1)S(1)} %constant_dynamic-slice_fusion.12, f32[4,512,2048]{2,1,0:T(8,128)} %get-tuple-element.325, f32[4,512]{1,0:T(4,128)S(1)} %get-tuple-element.324, pred[2048]{0:T(1024)(128)(4,1)S(1)} %add_compare_fusion.2), kind=kOutput, calls=%fused_computation.11.clone.1 | convolution fusion | flops 1094713344 | bytes 19933184 | tf_op jit(solution)/shard_map/while/body/eval_jaxpr/kqp,pkd->kqd/dot_general | solution.py:31
  113.6 1.6 bitcast_dynamic-update-slice_fusion.3
  116.0 1.5 dynamic_slice.82
  117.4 0.7 add_compare_fusion.2
  118.1 2.0 constant_dynamic-slice_fusion.9
  120.1 7.2 %fusion.81 = (f32[4,512]{1,0:T(4,128)S(1)}, f32[4,512,2048]{2,1,0:T(8,128)}) fusion(pred[2048]{0:T(1024)(128)(4,1)S(1)} %add_compare_fusion.2, bf16[1,2048,4,128]{3,2,1,0:T(4,128)(2,1)S(1)} %constant_dynamic-slice_fusion.9, bf16[4,64,32,128]{3,2,1,0:T(8,128)(2,1)S(1)} %copy-done, s32[]{:T(128)S(6)} %copy.150), kind=kOutput, calls=%fused_computation.3.clone.1 | convolution fusion | flops 1086322688 | bytes 19408900 | tf_op jit(solution)/shard_map/while/body/eval_jaxpr/kqd,pkd->kqp/dot_general | solution.py:24
  127.6 8.1 %fusion.82 = f32[4,512]{1,0:T(4,128)S(1)} fusion(f32[4,512,2048]{2,1,0:T(8,128)} %get-tuple-element.325, f32[4,512]{1,0:T(4,128)S(1)} %get-tuple-element.324, pred[2048]{0:T(1024)(128)(4,1)S(1)} %add_compare_fusion.2), kind=kLoop, calls=%fused_computation.5.clone.1 | loop fusion | flops 20969472 | bytes 16795648 | tf_op jit(solution)/shard_map/while/body/eval_jaxpr/reduce_sum | solution.py:30
  136.0 0.9 constant_dynamic-slice_fusion.10
  136.9 0.7 fusion.83
  139.2 0.9 constant_dynamic-slice_fusion.11
  140.0 0.4 convolution_bitcast_fusion.2
  140.4 2.0 constant_dynamic-slice_fusion.12
  142.4 7.7 %fusion.86 = f32[64,4,8,128]{3,2,0,1:T(8,128)S(1)} fusion(bf16[1,2048,4,128]{3,2,1,0:T(4,128)(2,1)S(1)} %constant_dynamic-slice_fusion.12, f32[4,512,2048]{2,1,0:T(8,128)} %get-tuple-element.325, f32[4,512]{1,0:T(4,128)S(1)} %get-tuple-element.324, pred[2048]{0:T(1024)(128)(4,1)S(1)} %add_compare_fusion.2), kind=kOutput, calls=%fused_computation.11.clone.1 | convolution fusion | flops 1094713344 | bytes 19933184 | tf_op jit(solution)/shard_map/while/body/eval_jaxpr/kqp,pkd->kqd/dot_general | solution.py:31
  150.1 1.6 bitcast_dynamic-update-slice_fusion.3
  152.6 63.0 %pmax.7 = f32[256,32]{0,1:T(8,128)S(1)} all-reduce(f32[256,32]{0,1:T(8,128)S(1)} %reshape.69), channel_id=1, replica_groups=mesh['seq'=16,'head'=2] {'seq'}, use_global_device_ids=true, to_apply=%region_6.7 | all-reduce | flops 8192 | bytes 65536 | tf_op jit(solution)/shard_map/pmax | solution.py:87
  215.7 0.8 copy.68
  216.6 4.1 %bitcast_multiply_fusion = f32[256,32,128]{2,1,0:T(8,128)} fusion(f32[4,64,32,128]{3,2,1,0:T(8,128)} %get-tuple-element.87, f32[256,32]{1,0:T(8,128)S(1)} %copy.63), kind=kLoop, calls=%fused_computation.55 | loop fusion | flops 1048576 | bytes 8421376 | tf_op jit(solution)/shard_map/mul | solution.py:91
  221.0 48.6 %reduce-scatter.10.cloned.1.call-done = f32[16,32]{1,0:T(8,128)} async-done(((f32[256,32]{1,0:T(8,128)}), f32[16,32]{1,0:T(8,128)}) %reduce-scatter.10.cloned.1.call-update) | async-done | bytes 2064
  269.5 0.8 copy.69
  270.5 74.7 %reduce-scatter.6.cloned.1.call-done = f32[16,32,128]{2,1,0:T(8,128)} async-done(((f32[256,32,128]{2,1,0:T(8,128)}), f32[16,32,128]{2,1,0:T(8,128)}) %reduce-scatter.6.cloned.1.call-update) | async-done | bytes 262160 | tf_op jit(solution)/shard_map/reduce_scatter | solution.py:91
  345.2 1.2 divide_convert_fusion
  346.4 0.7 copy.112
  347.2 40.7 %all-gather.2.cloned.1.call-done = bf16[256,4096]{1,0:T(8,128)(2,1)} async-done(((bf16[16,4096]{1,0:T(8,128)(2,1)}), bf16[256,4096]{1,0:T(8,128)(2,1)}) %all-gather.2.cloned.1.call-update) | async-done | bytes 2097168 | tf_op jit(solution)/shard_map/all_gather | solution.py:106
  387.9 4.9 %fusion.35 = f32[256,512]{1,0:T(8,128)} fusion(bf16[256,4096]{1,0:T(8,128)(2,1)} %all-gather.2.cloned.1.call-done, bf16[4096,512]{1,0:T(8,128)(2,1)} %param.17), kind=kOutput, calls=%fused_computation.63 | convolution fusion | flops 1073741824 | bytes 6815744 | tf_op jit(solution)/shard_map/dot_general | solution.py:108
  392.8 13.5 %reduce-scatter.8.cloned.1.call-done = f32[128,512]{1,0:T(8,128)} async-done(((f32[256,512]{1,0:T(8,128)}), f32[128,512]{1,0:T(8,128)}) %reduce-scatter.8.cloned.1.call-update) | async-done | bytes 262160 | tf_op jit(solution)/shard_map/reduce_scatter | solution.py:107
  406.3 1.6 convert_element_type.19
  (116 shorter events, 11.1 us)
Async XLA Ops:
  6.5 263.0 %reduce-scatter.10.cloned.1.call-start = ((), (), s32[]{:S(2)}) async-start(), calls=%async_computation.6 | async-start | bytes 139264
  6.6 4.2 %copy-start = (bf16[4,64,32,128]{3,2,1,0:T(8,128)(2,1)S(1)}, bf16[4,64,32,128]{3,2,1,0:T(8,128)(2,1)}, u32[]{:S(2)}) copy-start(bf16[4,64,32,128]{3,2,1,0:T(8,128)(2,1)} %get-tuple-element.372) | copy-start | bytes 6291460 | tf_op jit(solution)/shard_map/while
  43.0 4.2 %copy-start = (bf16[4,64,32,128]{3,2,1,0:T(8,128)(2,1)S(1)}, bf16[4,64,32,128]{3,2,1,0:T(8,128)(2,1)}, u32[]{:S(2)}) copy-start(bf16[4,64,32,128]{3,2,1,0:T(8,128)(2,1)} %get-tuple-element.372) | copy-start | bytes 6291460 | tf_op jit(solution)/shard_map/while
  79.5 4.2 %copy-start = (bf16[4,64,32,128]{3,2,1,0:T(8,128)(2,1)S(1)}, bf16[4,64,32,128]{3,2,1,0:T(8,128)(2,1)}, u32[]{:S(2)}) copy-start(bf16[4,64,32,128]{3,2,1,0:T(8,128)(2,1)} %get-tuple-element.372) | copy-start | bytes 6291460 | tf_op jit(solution)/shard_map/while
  116.0 4.2 %copy-start = (bf16[4,64,32,128]{3,2,1,0:T(8,128)(2,1)S(1)}, bf16[4,64,32,128]{3,2,1,0:T(8,128)(2,1)}, u32[]{:S(2)}) copy-start(bf16[4,64,32,128]{3,2,1,0:T(8,128)(2,1)} %get-tuple-element.372) | copy-start | bytes 6291460 | tf_op jit(solution)/shard_map/while
  216.5 128.7 %reduce-scatter.6.cloned.1.call-start = ((), (), s32[]{:S(2)}) async-start(), calls=%async_computation.3 | async-start | bytes 4456448 | tf_op jit(solution)/shard_map/reduce_scatter | solution.py:91
  220.8 167.1 %all-gather.2.cloned.1.call-start = ((), (), s32[]{:S(2)}) async-start(), calls=%async_computation.4 | async-start | bytes 2228224 | tf_op jit(solution)/shard_map/all_gather | solution.py:106
  347.2 59.1 %reduce-scatter.8.cloned.1.call-start = ((), (), s32[]{:S(2)}) async-start(), calls=%async_computation.5 | async-start | bytes 786432 | tf_op jit(solution)/shard_map/reduce_scatter | solution.py:107
Sparse Core Ops, SparseCore 0:
  216.6 52.8 reduce-scatter.9
  273.4 71.7 reduce-scatter.5
  347.4 40.4 all-gather.1
  392.9 13.3 reduce-scatter.7
where the time goes:
time: 416 us; the launch traced here: 414 us
  waiting for transfers between devices  178 us (43%)
  matrix products  71.1 us (17%)
  blocking collectives  63 us (15%)
  local copies, waits for them, and re-layouts  46 us (11%)
  other arithmetic  42.7 us (10%)
  between operations  13.2 us (3%)
    reduce_scatter x1, waiting for transfers between devices, body(): lax.psum_scatter(cache_acc * factor[..., None], 'seq', scatter_dimension=...  74.7 us
    pmax x1, blocking collectives, body(): overall = lax.pmax(cache_max, 'seq')  63 us
    unnamed x5, waiting for transfers between devices  48.6 us
    all_gather x1, waiting for transfers between devices, body(): attended = lax.all_gather(share, 'seq', axis=0, tiled=True)  40.7 us
    reduce_sum x8, other arithmetic, partial_scores(): totals = jnp.sum(weights, axis=-1)  32.9 us
    dot_general x8, matrix products, partial_scores(): jnp.einsum('kqp,pkd->kqd', weights.astype(jnp.bfloat16), values, preferre...  32.1 us
    dot_general x8, matrix products, partial_scores(): jnp.einsum('kqd,pkd->kqp', query_rows, keys, preferred_element_type=jnp.f...  30 us
    dynamic_slice x20, local copies, waits for them, and re-layouts, body(): lax.map(one_request, (queries, new_keys, new_values, cache_keys, cache_va...  28.8 us
  transfers between devices with their start and end apart: 4, of which 4 were waited for; matrix products, arithmetic and copies ran while one was open for 1% of the time, Pallas kernels for 0%

commit v1 on v0

v1 whole, which is shorter than its diff:
```python
import functools
import math

import jax
import jax.numpy as jnp
from jax import lax
from jax.experimental import pallas as pl
from jax.experimental.pallas import tpu as pltpu
from jax.sharding import PartitionSpec as P

lowest = -1e30
NT = (((1,), (1,)), ((), ()))
TN = (((0,), (0,)), ((), ()))


def bit_reversed(index, stages):
    result = index * 0
    for stage in range(stages):
        result = result * 2 + (index // (1 << stage)) % 2
    return result


def attend_kernel(kv_heads, split, stages, score_scale, lengths_ref, place_ref, q_ref, k_ref, v_ref,
                  tk_ref, tv_ref, parents_ref, o_ref, ml_ref):
    step = pl.program_id(0)
    block_size = k_ref.shape[0]
    columns = q_ref.shape[0]
    tile = min(256, columns)
    request = step // kv_heads
    me = place_ref[0]
    valid = lengths_ref[request] - me * block_size

    def write(masked):
        for start in range(0, columns, tile):
            here = pl.ds(start, tile)
            s = lax.dot_general(k_ref[...], q_ref[here, :], NT, preferred_element_type=jnp.float32)
            if masked:
                rows = lax.broadcasted_iota(jnp.int32, s.shape, 0)
                s = jnp.where(rows < valid, s, lowest)
            m = jnp.max(s, axis=0, keepdims=True) * score_scale
            w = jnp.exp2(s * score_scale - m)
            ml_ref[0, here] = m[0]
            ml_ref[1, here] = jnp.sum(w, axis=0)
            o_ref[:, here] = lax.dot_general(
                v_ref[...], w.astype(jnp.bfloat16), TN, preferred_element_type=jnp.float32
            ).astype(o_ref.dtype)

    @pl.when(valid >= block_size)
    def _():
        write(False)

    @pl.when((valid > 0) & (valid < block_size))
    def _():
        write(True)

    @pl.when(valid <= 0)
    def _():
        o_ref[...] = jnp.zeros_like(o_ref)
        ml_ref[0, :] = jnp.full((columns,), lowest, jnp.float32)
        ml_ref[1, :] = jnp.zeros((columns,), jnp.float32)

    own = bit_reversed(me, stages)

    @pl.when((own // split == step) & (own % split == 0))
    def _():
        tree = tk_ref.shape[0]

        def reach(parent_row):
            width = parent_row.shape[1]
            key = lax.broadcasted_iota(jnp.int32, (tree, width), 0)
            token = lax.broadcasted_iota(jnp.int32, (tree, width), 1) % tree
            hit = (parent_row == key) | (token == key)
            return jnp.where(hit, 1.0, 0.0)

        wide = reach(parents_ref[0:1, :])
        square = wide[:, :tree]
        for _ in range(max(1, (tree - 1).bit_length())):
            left = square.astype(jnp.bfloat16)
            wide = jnp.minimum(jnp.dot(left, wide.astype(jnp.bfloat16), preferred_element_type=jnp.float32), 1.0)
            square = wide[:, :tree]
        s = lax.dot_general(tk_ref[...], q_ref[...], NT, preferred_element_type=jnp.float32)
        allowed = wide > 0.5
        s = jnp.where(allowed, s * score_scale, lowest)
        m = jnp.max(s, axis=0, keepdims=True)
        w = jnp.where(allowed, jnp.exp2(s - m), 0.0)
        tot = jnp.sum(w, axis=0, keepdims=True)
        acc = lax.dot_general(tv_ref[...], w.astype(jnp.bfloat16), TN, preferred_element_type=jnp.float32)
        m_old = ml_ref[0:1, :]
        m_new = jnp.maximum(m_old, m)
        f_old, f_tree = jnp.exp2(m_old - m_new), jnp.exp2(m - m_new)
        ml_ref[1:2, :] = ml_ref[1:2, :] * f_old + tot * f_tree
        ml_ref[0:1, :] = m_new
        o_ref[...] = (o_ref[...].astype(jnp.float32) * f_old + acc * f_tree).astype(o_ref.dtype)


def merge_kernel(n, stages, split, turn, o_ref, ml_ref, g_ref, *scratch):
    per = 4
    o_cur = [o_ref] + list(scratch[0:stages])
    ml_cur = [ml_ref] + list(scratch[stages:2 * stages])
    o_in = scratch[2 * stages:3 * stages]
    ml_in = scratch[3 * stages:4 * stages]
    send, recv = scratch[4 * stages], scratch[4 * stages + 1]
    me = lax.axis_index("seq")
    bits = [(me // (1 << s)) % 2 for s in range(stages)]
    partners = [me + (1 - 2 * bits[s]) * (1 << s) for s in range(stages)]

    barrier = pltpu.get_barrier_semaphore()
    for s in range(stages):
        pl.semaphore_signal(barrier, inc=1, device_id={"seq": partners[s]}, device_id_type=pl.DeviceIdType.MESH)
    pl.semaphore_wait(barrier, stages)

    def remote(src, dst, slot, s):
        return pltpu.make_async_remote_copy(
            src_ref=src, dst_ref=dst, send_sem=send.at[slot], recv_sem=recv.at[slot],
            device_id={"seq": partners[s]}, device_id_type=pl.DeviceIdType.MESH,
        )

    waits = []
    for s in range(stages):
        half = n >> (s + 1)
        pairs = max(1, half // split)
        away, keep = (1 - bits[s]) * half, bits[s] * half
        pair_away, pair_keep = ((1 - bits[s]) * pairs, bits[s] * pairs) if half >= split else (0, 0)
        first = remote(o_cur[s].at[pl.ds(away, half)], o_in[s], 2 * s, s)
        second = remote(ml_cur[s].at[pl.ds(pair_away, pairs)], ml_in[s], 2 * s + 1, s)
        second.start()
        first.start()
        waits += [first, second]
        second.wait_recv()
        first.wait_recv()
        per_pair = half // pairs

        def one_pair(p, carry, s=s, keep=keep, pair_keep=pair_keep, per_pair=per_pair):
            m_a, m_b = ml_cur[s][pair_keep + p, 0:1, :], ml_in[s][p, 0:1, :]
            l_a, l_b = ml_cur[s][pair_keep + p, 1:2, :], ml_in[s][p, 1:2, :]
            m = jnp.maximum(m_a, m_b)
            f_a, f_b = jnp.exp2(m_a - m), jnp.exp2(m_b - m)
            ml_cur[s + 1][p, 0:1, :] = m
            ml_cur[s + 1][p, 1:2, :] = l_a * f_a + l_b * f_b
            for c in range(per_pair):
                at = p * per_pair + c
                mine = o_cur[s][keep + at].astype(jnp.float32)
                theirs = o_in[s][at].astype(jnp.float32)
                o_cur[s + 1][at] = (mine * f_a + theirs * f_b).astype(o_cur[s + 1].dtype)
            return carry

        lax.fori_loop(0, pairs, one_pair, 0)

    low = bit_reversed(me, stages)
    share = o_cur[stages][0].astype(jnp.float32) / ml_cur[stages][0, 1:2, :]
    if turn:
        share = share.T
    g_ref[low] = share.astype(g_ref.dtype)
    for s in reversed(range(stages)):
        size = n >> (s + 1)
        start = (low // size) * size
        block = g_ref.at[pl.ds(start, size)]
        copy = remote(block, block, 2 * stages + s, s)
        copy.start()
        waits.append(copy)
        copy.wait_recv()
    for copy in waits:
        copy.wait_send()


def body(queries, new_keys, new_values, cache_keys, cache_values, parents, kv_lengths, out_weight):
    requests, tree, heads, head_size = queries.shape
    kv_heads = new_keys.shape[2]
    group = heads // kv_heads
    block_size = cache_keys.shape[1]
    n = lax.axis_size("seq")
    stages = n.bit_length() - 1
    pairs = requests * kv_heads
    split = max(1, n // pairs)
    columns = group * tree
    deep = head_size * pairs // n
    me = lax.axis_index("seq")
    score_scale = math.log2(math.e) / math.sqrt(head_size)

    def by_head(array):
        return array.transpose(0, 2, 1, 3).reshape(pairs, array.shape[1], head_size)

    q = queries.reshape(requests, tree, kv_heads, group, head_size).transpose(0, 2, 3, 1, 4)
    q = q.reshape(pairs, columns, head_size)
    parent_rows = jnp.broadcast_to(jnp.tile(parents, (1, group))[:, None, :], (requests, 8, columns))

    def pair_block(rows):
        return pl.BlockSpec((None, rows, head_size), lambda p, *_: (p, 0, 0))

    o, ml = pl.pallas_call(
        functools.partial(attend_kernel, kv_heads, split, stages, score_scale),
        grid_spec=pltpu.PrefetchScalarGridSpec(
            num_scalar_prefetch=2,
            grid=(pairs,),
            in_specs=[
                pair_block(columns), pair_block(block_size), pair_block(block_size),
                pair_block(tree), pair_block(tree),
                pl.BlockSpec((None, 8, columns), lambda p, *_: (p // kv_heads, 0, 0)),
            ],
            out_specs=[
                pl.BlockSpec((None, head_size, columns), lambda p, *_: (p, 0, 0)),
                pl.BlockSpec((None, 2, columns), lambda p, *_: (p, 0, 0)),
            ],
        ),
        out_shape=[
            jax.ShapeDtypeStruct((pairs, head_size, columns), jnp.bfloat16),
            jax.ShapeDtypeStruct((pairs, 2, columns), jnp.float32),
        ],
        compiler_params=pltpu.CompilerParams(vmem_limit_bytes=48 * 1024 * 1024),
    )(kv_lengths, me[None].astype(jnp.int32), q, by_head(cache_keys), by_head(cache_values),
      by_head(new_keys), by_head(new_values), parent_rows)

    turn = split == 1 and deep == head_size
    o = o.reshape(n, deep, columns)
    piece = (columns, deep) if turn else (deep, columns)
    halves = [n >> (s + 1) for s in range(stages)]
    o_bufs = [pltpu.VMEM((h, deep, columns), jnp.bfloat16) for h in halves]
    ml_bufs = [pltpu.VMEM((max(1, h // split), 2, columns), jnp.float32) for h in halves]
    vmem = pl.BlockSpec(memory_space=pltpu.VMEM)
    gathered = pl.pallas_call(
        functools.partial(merge_kernel, n, stages, split, turn),
        out_shape=jax.ShapeDtypeStruct((n,) + piece, jnp.bfloat16),
        in_specs=[vmem, vmem],
        out_specs=vmem,
        scratch_shapes=o_bufs + ml_bufs + o_bufs + ml_bufs
        + [pltpu.SemaphoreType.DMA((3 * stages,)), pltpu.SemaphoreType.DMA((3 * stages,))],
        compiler_params=pltpu.CompilerParams(
            collective_id=0, has_side_effects=True, vmem_limit_bytes=32 * 1024 * 1024
        ),
    )(o, ml)
    if turn:
        attended = gathered.reshape(requests, kv_heads, group, tree, head_size).transpose(0, 3, 1, 2, 4)
    else:
        attended = gathered.reshape(requests, kv_heads, head_size, group, tree).transpose(0, 4, 1, 3, 2)
    attended = attended.reshape(requests * tree, heads * head_size)
    mixed = lax.psum_scatter(
        jnp.dot(attended, out_weight, preferred_element_type=jnp.float32),
        "head",
        scatter_dimension=0,
        tiled=True,
    )
    return mixed.astype(jnp.bfloat16)


def solution(mesh):
    placed = (
        P(None, None, "head", None),
        P(None, None, "head", None),
        P(None, None, "head", None),
        P(None, "seq", "head", None),
        P(None, "seq", "head", None),
        P(),
        P(),
        P("head", "seq"),
    )
    return jax.shard_map(
        body, mesh=mesh, in_specs=placed, out_specs=P("head", "seq"), check_vma=False
    )
```

time: 416 us -> 167 us (0.40)
  waiting for transfers between devices: 178 us -> 16.9 us
  Pallas kernels: 0 us -> 104 us
  matrix products: 71.1 us -> 4.85 us
  blocking collectives: 63 us -> 0 us
  other arithmetic: 42.7 us -> 1.62 us
  local copies, waits for them, and re-layouts: 46 us -> 25.4 us
    pallas_call x0 -> x2, Pallas kernels: none -> 104 us  [the longest x1 57.1 us: body(): pl.pallas_call(functools.partial(merge_kernel, n, stages, split, turn), o...]
    reduce_scatter x1 -> x0, waiting for transfers between devices: 74.7 us -> none  [body(): lax.psum_scatter(cache_acc * factor[..., None], 'seq', scatter_dimension=...]
    dot_general x40 -> x0, matrix products: 66.3 us -> none  [the longest x8 32.1 us: partial_scores(): jnp.einsum('kqp,pkd->kqd', weights.astype(jnp.bfloat16), values, preferre...]
    pmax x1 -> x0, blocking collectives: 63 us -> none  [body(): overall = lax.pmax(cache_max, 'seq')]
    unnamed x5 -> x1, waiting for transfers between devices: 48.6 us -> 0.02 us
    all_gather x1 -> x0, waiting for transfers between devices: 40.7 us -> none  [body(): attended = lax.all_gather(share, 'seq', axis=0, tiled=True)]
    reduce_sum x8 -> x0, other arithmetic: 32.9 us -> none  [partial_scores(): totals = jnp.sum(weights, axis=-1)]
    dynamic_slice x20 -> x0, local copies, waits for them, and re-layouts: 28.8 us -> none  [body(): lax.map(one_request, (queries, new_keys, new_values, cache_keys, cache_va...]
  transfers between devices with their start and end apart: 4 -> 1, of which waited for: 4 -> 1; matrix products, arithmetic and copies ran while one was open for 1% -> 0% of each run, Pallas kernels for 0% -> 0%
where the time goes in v1:
time: 167 us; the launch traced here: 166 us
  Pallas kernels  104 us (62%)
  local copies, waits for them, and re-layouts  25.4 us (15%)
  waiting for transfers between devices  16.9 us (10%)
  between operations  13.4 us (8%)
  matrix products  4.85 us (3%)
    pallas_call x1, Pallas kernels, body(): pl.pallas_call(functools.partial(merge_kernel, n, stages, split, turn), o...  57.1 us
    pallas_call x1, Pallas kernels, body(): pl.pallas_call(functools.partial(attend_kernel, kv_heads, split, stages,...  47.1 us
    transpose x4, local copies, waits for them, and re-layouts, by_head(): return array.transpose(0, 2, 1, 3).reshape(pairs, array.shape[1], head_size)  18.5 us
    reduce_scatter x1, waiting for transfers between devices, body(): lax.psum_scatter(jnp.dot(attended, out_weight, preferred_element_type=jnp...  16.8 us
    dot_general x1, matrix products, body(): jnp.dot(attended, out_weight, preferred_element_type=jnp.float32)  4.85 us
  transfers between devices with their start and end apart: 1, of which 1 were waited for; matrix products, arithmetic and copies ran while one was open for 0% of the time, Pallas kernels for 0%

profile of v1, /device:TPU:0, one launch (start us, length us, event | category | flops | bytes accessed | tf_op | source)
XLA Modules:
  0.0 166.4 jit_solution(10940686994352450635)
XLA Ops:
  6.5 0.0 reduce-scatter.2.cloned.1.call-start
  6.5 0.7 tile.8
  7.2 0.1 tile.9
  7.3 1.0 copy.17
  8.3 1.0 copy.18
  9.3 2.4 %copy.14 = bf16[4,64,4,8,128]{4,1,3,2,0:T(8,128)(2,1)S(1)} copy(bf16[4,64,4,8,128]{4,3,2,1,0:T(8,128)(2,1)} %bitcast.30) | data formatting | bytes 4194304 | tf_op jit(solution)/shard_map/reshape | solution.py:183
  11.7 8.3 %copy.15 = bf16[4,4,2048,128]{3,2,1,0:T(8,128)(2,1)} copy(bf16[4,4,2048,128]{3,1,2,0:T(4,128)(2,1)} %bitcast.27) | data formatting | bytes 16777216 | tf_op jit(solution)/shard_map/transpose | solution.py:181
  20.0 0.0 copy-start
  20.0 8.3 %copy.16 = bf16[4,4,2048,128]{3,2,1,0:T(8,128)(2,1)} copy(bf16[4,4,2048,128]{3,1,2,0:T(4,128)(2,1)} %bitcast.28) | data formatting | bytes 16777216 | tf_op jit(solution)/shard_map/transpose | solution.py:181
  28.3 0.0 copy-done
  28.3 47.1 %shard_map.82 = (bf16[16,128,512]{2,1,0:T(8,128)(2,1)S(1)}, f32[16,2,512]{2,1,0:T(2,128)S(1)}) custom-call(s32[4]{0:T(128)S(1)} %copy-done, s32[1]{0:T(128)} %bitcast.place_ref, bf16[16,512,128]{2,1,0:T(8,128)(2,1)S(1)} %bitcast.21, bf16[16,2048,128]{2,1,0:T(8,128)(2,1)} %bitcast.25, bf16[16,2048,128]{2,1,0:T(8,128)(2,1)} %bitcast.26, ...), custom_call_target="tpu_custom_call" | custom-call | tf_op jit(solution)/shard_map/pallas_call | solution.py:190
  75.4 57.1 %shard_map.83 = bf16[16,512,128]{2,1,0:T(8,128)(2,1)S(1)} custom-call(bf16[16,128,512]{2,1,0:T(8,128)(2,1)S(1)} %get-tuple-element.7.o_ref, f32[16,2,512]{2,1,0:T(2,128)S(1)} %get-tuple-element.8.ml_ref), custom_call_target="tpu_custom_call" | custom-call | tf_op jit(solution)/shard_map/pallas_call | solution.py:220
  132.5 1.4 copy.21
  133.9 2.3 %reshape.37 = bf16[256,4096]{1,0:T(8,128)(2,1)} reshape(bf16[4,64,4,8,128]{4,3,2,1,0:T(8,128)(2,1)S(1)} %bitcast.29) | data formatting | bytes 4194304 | tf_op jit(solution)/shard_map/reshape | solution.py:235
  136.2 4.9 %fusion = f32[256,512]{1,0:T(8,128)} fusion(bf16[256,4096]{1,0:T(8,128)(2,1)} %reshape.37, bf16[4096,512]{1,0:T(8,128)(2,1)} %param.15), kind=kOutput, calls=%fused_computation.1 | convolution fusion | flops 1073741824 | bytes 6815744 | tf_op jit(solution)/shard_map/dot_general | solution.py:237
  141.0 0.0 reduce-scatter.2.cloned.1.call-update
  141.0 16.8 %reduce-scatter.2.cloned.1.call-done = f32[128,512]{1,0:T(8,128)} async-done(((f32[256,512]{1,0:T(8,128)}), f32[128,512]{1,0:T(8,128)}) %reduce-scatter.2.cloned.1.call-update) | async-done | bytes 262160 | tf_op jit(solution)/shard_map/reduce_scatter | solution.py:236
  157.9 1.6 convert_element_type.3
  (1 shorter events, 0.0 us)
Async XLA Ops:
  6.5 151.4 %reduce-scatter.2.cloned.1.call-start = ((), (), s32[]{:S(2)}) async-start(), calls=%async_computation.1 | async-start | bytes 786432 | tf_op jit(solution)/shard_map/reduce_scatter | solution.py:236
  20.0 8.3 %copy-start = (s32[4]{0:T(128)S(1)}, s32[4]{0:T(128)}, u32[]{:S(2)}) copy-start(s32[4]{0:T(128)} %lengths_ref.1) | copy-start | bytes 52
Sparse Core Ops, SparseCore 0:
  141.2 16.6 reduce-scatter.1

commit v2 on v1

v2 whole, which is shorter than its diff:
```python
import functools
import math

import jax
import jax.numpy as jnp
from jax import lax
from jax.experimental import pallas as pl
from jax.experimental.pallas import tpu as pltpu
from jax.sharding import PartitionSpec as P

lowest = -1e30
NT = (((1,), (1,)), ((), ()))
TN = (((0,), (0,)), ((), ()))


def bit_reversed(index, stages):
    result = index * 0
    for stage in range(stages):
        result = result * 2 + (index // (1 << stage)) % 2
    return result


def attend_kernel(kv_heads, split, stages, score_scale, lengths_ref, place_ref, q_ref, k_ref, v_ref,
                  tk_ref, tv_ref, parents_ref, o_ref, ml_ref):
    step = pl.program_id(0)
    block_size = k_ref.shape[0]
    columns = q_ref.shape[0]
    tile = min(256, columns)
    streams, _, lanes = o_ref.shape
    request = step // kv_heads
    me = place_ref[0]
    valid = lengths_ref[request] - me * block_size

    def write(masked):
        for start in range(0, columns, tile):
            here = pl.ds(start, tile)
            s = lax.dot_general(k_ref[...], q_ref[here, :], NT, preferred_element_type=jnp.float32)
            if masked:
                rows = lax.broadcasted_iota(jnp.int32, s.shape, 0)
                s = jnp.where(rows < valid, s, lowest)
            m = jnp.max(s, axis=0, keepdims=True) * score_scale
            w = jnp.exp2(s * score_scale - m)
            tot = jnp.sum(w, axis=0, keepdims=True)
            acc = lax.dot_general(
                v_ref[...], w.astype(jnp.bfloat16), TN, preferred_element_type=jnp.float32
            ).astype(o_ref.dtype)
            for inner in range(0, tile, lanes):
                t = (start + inner) // lanes
                ml_ref[t, 0:1, :] = m[:, inner:inner + lanes]
                ml_ref[t, 1:2, :] = tot[:, inner:inner + lanes]
                o_ref[t] = acc[:, inner:inner + lanes]

    @pl.when(valid >= block_size)
    def _():
        write(False)

    @pl.when((valid > 0) & (valid < block_size))
    def _():
        write(True)

    @pl.when(valid <= 0)
    def _():
        o_ref[...] = jnp.zeros_like(o_ref)
        ml_ref[:, 0:1, :] = jnp.full((streams, 1, lanes), lowest, jnp.float32)
        ml_ref[:, 1:2, :] = jnp.zeros((streams, 1, lanes), jnp.float32)

    own = bit_reversed(me, stages)

    @pl.when((own // split == step) & (own % split == 0))
    def _():
        tree = tk_ref.shape[0]

        def reach(parent_row):
            width = parent_row.shape[1]
            key = lax.broadcasted_iota(jnp.int32, (tree, width), 0)
            token = lax.broadcasted_iota(jnp.int32, (tree, width), 1) % tree
            hit = (parent_row == key) | (token == key)
            return jnp.where(hit, 1.0, 0.0)

        wide = reach(parents_ref[0:1, :])
        square = wide[:, :tree]
        for _ in range(max(1, (tree - 1).bit_length())):
            left = square.astype(jnp.bfloat16)
            wide = jnp.minimum(jnp.dot(left, wide.astype(jnp.bfloat16), preferred_element_type=jnp.float32), 1.0)
            square = wide[:, :tree]
        s = lax.dot_general(tk_ref[...], q_ref[...], NT, preferred_element_type=jnp.float32)
        allowed = wide > 0.5
        s = jnp.where(allowed, s * score_scale, lowest)
        m = jnp.max(s, axis=0, keepdims=True)
        w = jnp.where(allowed, jnp.exp2(s - m), 0.0)
        tot = jnp.sum(w, axis=0, keepdims=True)
        acc = lax.dot_general(tv_ref[...], w.astype(jnp.bfloat16), TN, preferred_element_type=jnp.float32)
        for t in range(streams):
            here = slice(t * lanes, (t + 1) * lanes)
            m_old = ml_ref[t, 0:1, :]
            m_new = jnp.maximum(m_old, m[:, here])
            f_old, f_tree = jnp.exp2(m_old - m_new), jnp.exp2(m[:, here] - m_new)
            ml_ref[t, 1:2, :] = ml_ref[t, 1:2, :] * f_old + tot[:, here] * f_tree
            ml_ref[t, 0:1, :] = m_new
            o_ref[t] = (o_ref[t].astype(jnp.float32) * f_old + acc[:, here] * f_tree).astype(o_ref.dtype)


def merge_kernel(n, stages, split, orders, masks, head_axis, fused, o_ref, ml_ref, *refs):
    streams = len(orders)
    if fused:
        w_ref, out_ref, *scratch = refs
    else:
        g_ref, *scratch = refs
    scratch = list(scratch)

    def take(count):
        taken = scratch[:count]
        del scratch[:count]
        return taken

    o_sum, o_out, o_in, ml_out, ml_in = (take(stages) for _ in range(5))
    (send, recv) = take(2)
    me = lax.axis_index("seq")

    def bit(position):
        return (me // (1 << position)) % 2

    partners, bits = [], []
    for position in range(stages):
        move = 0
        for q in range(stages):
            if (masks[position] >> q) & 1:
                move = move + (1 - 2 * bit(q)) * (1 << q)
        partners.append(me + move)
        value = bit(position)
        for other in range(position + 1, stages):
            if (masks[other] >> position) & 1:
                value = (value + bit(other)) % 2
        bits.append(value)

    head_stages = []
    if fused:
        (attended, product) = take(2)
        head_count = lax.axis_size(head_axis)
        head_stages = take(head_count.bit_length() - 1)
        (head_send, head_recv) = take(2)
        head = lax.axis_index(head_axis)

    barrier = pltpu.get_barrier_semaphore()
    for partner in partners:
        pl.semaphore_signal(barrier, inc=1, device_id={"seq": partner}, device_id_type=pl.DeviceIdType.MESH)
    head_plan = []
    for s in range(len(head_stages)):
        stride = head_count >> (s + 1)
        head_bit = (head // stride) % 2
        partner = head + (1 - 2 * head_bit) * stride
        head_plan.append((head_bit, partner))
        pl.semaphore_signal(barrier, inc=1, device_id={head_axis: partner}, device_id_type=pl.DeviceIdType.MESH)
    pl.semaphore_wait(barrier, stages + len(head_stages))

    def remote(src, dst, slot, position):
        return pltpu.make_async_remote_copy(
            src_ref=src, dst_ref=dst, send_sem=send.at[slot], recv_sem=recv.at[slot],
            device_id={"seq": partners[position]}, device_id_type=pl.DeviceIdType.MESH,
        )

    waits = []
    flying = {}

    def begin(t, s):
        position = orders[t][s]
        half = n >> (s + 1)
        pairs = max(1, half // split)
        away = (1 - bits[position]) * half
        pair_away = (1 - bits[position]) * pairs if half >= split else 0
        o_src = o_ref if s == 0 else o_out[s - 1]
        ml_src = ml_ref if s == 0 else ml_out[s - 1]
        slot = (t * stages + s) * 3
        small = remote(ml_src.at[t, pl.ds(pair_away, pairs)], ml_in[s].at[t], slot, position)
        large = remote(o_src.at[t, pl.ds(away, half)], o_in[s].at[t], slot + 1, position)
        small.start()
        large.start()
        waits.extend([small, large])
        flying[t] = (small, large)

    def finish(t, s):
        position = orders[t][s]
        half = n >> (s + 1)
        pairs = max(1, half // split)
        keep = bits[position] * half
        pair_keep = bits[position] * pairs if half >= split else 0
        per_pair = half // pairs
        small, large = flying[t]
        small.wait_recv()
        large.wait_recv()
        ml_src = ml_ref if s == 0 else ml_out[s - 1]
        o_src = o_ref if s == 0 else o_sum[s - 1]

        def one_pair(p, carry):
            m_a, m_b = ml_src[t, pair_keep + p, 0:1, :], ml_in[s][t, p, 0:1, :]
            l_a, l_b = ml_src[t, pair_keep + p, 1:2, :], ml_in[s][t, p, 1:2, :]
            m = jnp.maximum(m_a, m_b)
            f_a, f_b = jnp.exp2(m_a - m), jnp.exp2(m_b - m)
            ml_out[s][t, p, 0:1, :] = m
            ml_out[s][t, p, 1:2, :] = l_a * f_a + l_b * f_b
            for c in range(per_pair):
                at = p * per_pair + c
                mine = o_src[t, keep + at].astype(jnp.float32)
                theirs = o_in[s][t, at].astype(jnp.float32)
                total = mine * f_a + theirs * f_b
                o_sum[s][t, at] = total
                o_out[s][t, at] = total.astype(jnp.bfloat16)
            return carry

        lax.fori_loop(0, pairs, one_pair, 0)

    for t in range(streams):
        begin(t, 0)
    lows = [0] * streams
    gathered = attended if fused else g_ref

    def gather(t, s):
        size = n >> (s + 1)
        start = (lows[t] // size) * size
        block = gathered.at[t, pl.ds(start, size)]
        copy = remote(block, block, (t * stages + s) * 3 + 2, orders[t][s])
        copy.start()
        waits.append(copy)
        flying[t] = copy

    for s in range(stages):
        for t in range(streams):
            finish(t, s)
            if s + 1 < stages:
                begin(t, s + 1)
            else:
                low = 0
                for position in orders[t]:
                    low = low * 2 + bits[position]
                lows[t] = low
                share = o_sum[s][t, 0] / ml_out[s][t, 0, 1:2, :]
                if fused:
                    share = share.T
                gathered[t, low] = share.astype(jnp.bfloat16)
                gather(t, s)
    for s in reversed(range(stages)):
        for t in range(streams):
            flying[t].wait_recv()
            if s > 0:
                gather(t, s - 1)

    if fused:
        tokens, width = product.shape
        requests, tree = fused
        kv_heads = n // requests
        parts = attended.shape[2] // tree
        groups = streams * parts
        head_size = attended.shape[3]

        def rows_of(request):
            pieces = []
            for k in range(kv_heads):
                for t in range(streams):
                    for g in range(parts):
                        pieces.append(attended[t, request * kv_heads + k, g * tree:(g + 1) * tree, :])
            return jnp.concatenate(pieces, axis=1)

        half = tokens // 2
        per_half = requests // 2
        copies = []

        def head_copy(s, start, rows):
            copy = pltpu.make_async_remote_copy(
                src_ref=product.at[pl.ds(start, rows)], dst_ref=head_stages[s],
                send_sem=head_send.at[s], recv_sem=head_recv.at[s],
                device_id={head_axis: head_plan[s][1]}, device_id_type=pl.DeviceIdType.MESH,
            )
            copy.start()
            copies.append(copy)
            return copy

        first_bit = head_plan[0][0]
        for turn in range(2):
            side = (1 - first_bit) if turn == 0 else first_bit
            rows = jnp.concatenate([rows_of(side * per_half + q) for q in range(per_half)], axis=0)
            product[pl.ds(side * half, half), :] = jnp.dot(
                rows, w_ref[...], preferred_element_type=jnp.float32)
            if turn == 0:
                copy = head_copy(0, side * half, half)
        base, size = first_bit * half, half
        for s in range(len(head_stages)):
            if s > 0:
                size = size // 2
                copy = head_copy(s, base + (1 - head_plan[s][0]) * size, size)
                base = base + head_plan[s][0] * size
            copy.wait_recv()
            total = product[pl.ds(base, size), :] + head_stages[s][...]
            if s + 1 < len(head_stages):
                product[pl.ds(base, size), :] = total
            else:
                out_ref[...] = total.astype(out_ref.dtype)
        for copy in copies:
            copy.wait_send()
    for copy in waits:
        copy.wait_send()


def body(queries, new_keys, new_values, cache_keys, cache_values, parents, kv_lengths, out_weight):
    requests, tree, heads, head_size = queries.shape
    kv_heads = new_keys.shape[2]
    group = heads // kv_heads
    block_size = cache_keys.shape[1]
    n = lax.axis_size("seq")
    stages = n.bit_length() - 1
    pairs = requests * kv_heads
    split = max(1, n // pairs)
    columns = group * tree
    deep = head_size * pairs // n
    lanes = min(128, columns)
    streams = columns // lanes
    me = lax.axis_index("seq")
    score_scale = math.log2(math.e) / math.sqrt(head_size)

    def by_head(array):
        return array.transpose(0, 2, 1, 3).reshape(pairs, array.shape[1], head_size)

    q = queries.reshape(requests, tree, kv_heads, group, head_size).transpose(0, 2, 3, 1, 4)
    q = q.reshape(pairs, columns, head_size)
    parent_rows = jnp.broadcast_to(jnp.tile(parents, (1, group))[:, None, :], (requests, 8, columns))

    def pair_block(rows):
        return pl.BlockSpec((None, rows, head_size), lambda p, *_: (p, 0, 0))

    o, ml = pl.pallas_call(
        functools.partial(attend_kernel, kv_heads, split, stages, score_scale),
        grid_spec=pltpu.PrefetchScalarGridSpec(
            num_scalar_prefetch=2,
            grid=(pairs,),
            in_specs=[
                pair_block(columns), pair_block(block_size), pair_block(block_size),
                pair_block(tree), pair_block(tree),
                pl.BlockSpec((None, 8, columns), lambda p, *_: (p // kv_heads, 0, 0)),
            ],
            out_specs=[
                pl.BlockSpec((streams, None, head_size, lanes), lambda p, *_: (0, p, 0, 0)),
                pl.BlockSpec((streams, None, 2, lanes), lambda p, *_: (0, p, 0, 0)),
            ],
        ),
        out_shape=[
            jax.ShapeDtypeStruct((streams, pairs, head_size, lanes), jnp.bfloat16),
            jax.ShapeDtypeStruct((streams, pairs, 2, lanes), jnp.float32),
        ],
        compiler_params=pltpu.CompilerParams(vmem_limit_bytes=48 * 1024 * 1024),
    )(kv_lengths, me[None].astype(jnp.int32), q, by_head(cache_keys), by_head(cache_values),
      by_head(new_keys), by_head(new_values), parent_rows)

    fused = (requests, tree) if n == pairs and lanes == head_size else None
    o = o.reshape(streams, n, deep, lanes)
    halves = [n >> (s + 1) for s in range(stages)]
    masks = [1 << s for s in range(stages)]
    if stages > 3:
        masks[3] = 12
    order = list(range(stages))
    turned = order[:1] + order[2:] + order[1:2]
    orders = [turned if t % 2 else order for t in range(streams)]

    def buffers(rows, kind):
        return [pltpu.VMEM((streams, h, rows, lanes), kind) for h in halves]

    ml_bufs = [pltpu.VMEM((streams, max(1, h // split), 2, lanes), jnp.float32) for h in halves]
    scratch = (buffers(deep, jnp.float32) + buffers(deep, jnp.bfloat16) + buffers(deep, jnp.bfloat16)
               + ml_bufs + ml_bufs + [pltpu.SemaphoreType.DMA((3 * stages * streams,))] * 2)
    vmem = pl.BlockSpec(memory_space=pltpu.VMEM)
    params = pltpu.CompilerParams(collective_id=0, has_side_effects=True, vmem_limit_bytes=48 * 1024 * 1024)
    if fused:
        tokens, width = requests * tree, out_weight.shape[1]
        count = lax.axis_size("head")
        head_bufs = [pltpu.VMEM((tokens >> (s + 1), width), jnp.float32) for s in range(count.bit_length() - 1)]
        return pl.pallas_call(
            functools.partial(merge_kernel, n, stages, split, orders, masks, "head", fused),
            out_shape=jax.ShapeDtypeStruct((tokens // count, width), jnp.bfloat16),
            in_specs=[vmem, vmem, vmem],
            out_specs=vmem,
            scratch_shapes=scratch
            + [pltpu.VMEM((streams, n, lanes, head_size), jnp.bfloat16), pltpu.VMEM((tokens, width), jnp.float32)]
            + head_bufs + [pltpu.SemaphoreType.DMA((len(head_bufs),))] * 2,
            compiler_params=params,
        )(o, ml, out_weight)
    gathered = pl.pallas_call(
        functools.partial(merge_kernel, n, stages, split, orders, masks, "head", fused),
        out_shape=jax.ShapeDtypeStruct((streams, n, deep, lanes), jnp.bfloat16),
        in_specs=[vmem, vmem],
        out_specs=vmem,
        scratch_shapes=scratch,
        compiler_params=params,
    )(o, ml)
    attended = gathered.reshape(streams, requests, kv_heads, head_size, lanes).transpose(1, 2, 0, 4, 3)
    attended = attended.reshape(requests, kv_heads, group, tree, head_size).transpose(0, 3, 1, 2, 4)
    attended = attended.reshape(requests * tree, heads * head_size)
    mixed = lax.psum_scatter(
        jnp.dot(attended, out_weight, preferred_element_type=jnp.float32),
        "head",
        scatter_dimension=0,
        tiled=True,
    )
    return mixed.astype(jnp.bfloat16)


def solution(mesh):
    placed = (
        P(None, None, "head", None),
        P(None, None, "head", None),
        P(None, None, "head", None),
        P(None, "seq", "head", None),
        P(None, "seq", "head", None),
        P(),
        P(),
        P("head", "seq"),
    )
    return jax.shard_map(
        body, mesh=mesh, in_specs=placed, out_specs=P("head", "seq"), check_vma=False
    )
```

time: 167 us -> 121 us (0.72)
  waiting for transfers between devices: 16.9 us -> 0 us
  between operations: 13.4 us -> 0.04 us
  Pallas kernels: 104 us -> 98.2 us
  matrix products: 4.85 us -> 0 us
  local copies, waits for them, and re-layouts: 25.4 us -> 22.3 us
    reduce_scatter x1 -> x0, waiting for transfers between devices: 16.8 us -> none  [body(): lax.psum_scatter(jnp.dot(attended, out_weight, preferred_element_type=jnp...]
    pallas_call x1, Pallas kernels: 57.1 us -> 49.5 us  [body(): pl.pallas_call(functools.partial(merge_kernel, n, stages, split, orders,...]
    dot_general x1 -> x0, matrix products: 4.85 us -> none  [body(): jnp.dot(attended, out_weight, preferred_element_type=jnp.float32)]
    reshape x2 -> x0, local copies, waits for them, and re-layouts: 3.66 us -> none  [the longest x1 2.3 us: body(): attended = attended.reshape(requests * tree, heads * head_size)]
  transfers between devices with their start and end apart: 1 -> 0, of which waited for: 1 -> 0; matrix products, arithmetic and copies ran while one was open for 0% -> 0% of each run, Pallas kernels for 0% -> 0%
where the time goes in v2:
time: 121 us
  Pallas kernels  98.2 us (81%)
  local copies, waits for them, and re-layouts  22.3 us (18%)
    pallas_call x1, Pallas kernels, body(): pl.pallas_call(functools.partial(merge_kernel, n, stages, split, orders,...  49.5 us
    pallas_call x1, Pallas kernels, body(): pl.pallas_call(functools.partial(attend_kernel, kv_heads, split, stages,...  48.7 us
    transpose x4, local copies, waits for them, and re-layouts, by_head(): return array.transpose(0, 2, 1, 3).reshape(pairs, array.shape[1], head_size)  18.5 us

profile of v2, /device:TPU:0, one launch (start us, length us, event | category | flops | bytes accessed | tf_op | source)
XLA Modules:
  0.0 120.6 jit_solution(6609426378609818458)
XLA Ops:
  0.0 0.7 tile.8
  0.7 0.1 tile.9
  0.8 1.0 copy.12
  1.8 1.0 copy.13
  2.8 2.4 %copy.9 = bf16[4,64,4,8,128]{4,1,3,2,0:T(8,128)(2,1)S(1)} copy(bf16[4,64,4,8,128]{4,3,2,1,0:T(8,128)(2,1)} %bitcast.20) | data formatting | bytes 4194304 | tf_op jit(solution)/shard_map/reshape | solution.py:322
  5.2 8.2 %copy.10 = bf16[4,4,2048,128]{3,2,1,0:T(8,128)(2,1)} copy(bf16[4,4,2048,128]{3,1,2,0:T(4,128)(2,1)} %bitcast.18) | data formatting | bytes 16777216 | tf_op jit(solution)/shard_map/transpose | solution.py:320
  13.4 0.0 copy-start
  13.4 8.3 %copy.11 = bf16[4,4,2048,128]{3,2,1,0:T(8,128)(2,1)} copy(bf16[4,4,2048,128]{3,1,2,0:T(4,128)(2,1)} %bitcast.19) | data formatting | bytes 16777216 | tf_op jit(solution)/shard_map/transpose | solution.py:320
  21.7 0.0 copy-done
  21.7 48.7 %shard_map.82 = (bf16[4,16,128,128]{3,2,1,0:T(8,128)(2,1)S(1)}, f32[4,16,2,128]{3,2,1,0:T(2,128)S(1)}) custom-call(s32[4]{0:T(128)S(1)} %copy-done, s32[1]{0:T(128)} %bitcast.place_ref, bf16[16,512,128]{2,1,0:T(8,128)(2,1)S(1)} %bitcast.13, bf16[16,2048,128]{2,1,0:T(8,128)(2,1)} %bitcast.16, bf16[16,2048,128]{2,1,0:T(8,128)(2,1)} %bitcast.17, ...), custom_call_target="tpu_custom_call" | custom-call | tf_op jit(solution)/shard_map/pallas_call | solution.py:329
  70.4 49.5 %shard_map.83 = bf16[128,512]{1,0:T(8,128)(2,1)S(1)} custom-call(bf16[4,16,128,128]{3,2,1,0:T(8,128)(2,1)S(1)} %get-tuple-element.7.o_ref, f32[4,16,2,128]{3,2,1,0:T(2,128)S(1)} %get-tuple-element.8.ml_ref, bf16[4096,512]{1,0:T(8,128)(2,1)} %refs_0_.1), custom_call_target="tpu_custom_call" | custom-call | tf_op jit(solution)/shard_map/pallas_call | solution.py:374
  119.9 0.7 copy.15
  (1 shorter events, 0.0 us)
Async XLA Ops:
  13.4 8.3 %copy-start = (s32[4]{0:T(128)S(1)}, s32[4]{0:T(128)}, u32[]{:S(2)}) copy-start(s32[4]{0:T(128)} %lengths_ref.1) | copy-start | bytes 52

commit v3 on v2

--- a/solution.py
+++ b/solution.py
@@ -21,20 +21,34 @@
 
 
 def attend_kernel(kv_heads, split, stages, score_scale, lengths_ref, place_ref, q_ref, k_ref, v_ref,
-                  tk_ref, tv_ref, parents_ref, o_ref, ml_ref):
+                  tk_ref, tv_ref, parents_ref, o_ref, ml_ref, *scratch):
     step = pl.program_id(0)
     block_size = k_ref.shape[0]
+    head = step % kv_heads
     columns = q_ref.shape[0]
-    tile = min(256, columns)
+    tile = columns
     streams, _, lanes = o_ref.shape
     request = step // kv_heads
     me = place_ref[0]
     valid = lengths_ref[request] - me * block_size
+    if scratch:
+        keys_ref, values_ref, tree_keys_ref, tree_values_ref = scratch
+
+        @pl.when((head == 0) & (valid > 0))
+        def _():
+            keys_ref[...] = jnp.swapaxes(k_ref[...], 0, 1)
+            values_ref[...] = jnp.swapaxes(v_ref[...], 0, 1)
+
+    def keys_of(ref, split_ref):
+        return split_ref[head] if scratch else ref[...]
+
+    if not scratch:
+        keys_ref = values_ref = tree_keys_ref = tree_values_ref = None
 
     def write(masked):
         for start in range(0, columns, tile):
             here = pl.ds(start, tile)
-            s = lax.dot_general(k_ref[...], q_ref[here, :], NT, preferred_element_type=jnp.float32)
+            s = lax.dot_general(keys_of(k_ref, keys_ref), q_ref[here, :], NT, preferred_element_type=jnp.float32)
             if masked:
                 rows = lax.broadcasted_iota(jnp.int32, s.shape, 0)
                 s = jnp.where(rows < valid, s, lowest)
@@ -42,7 +56,7 @@
             w = jnp.exp2(s * score_scale - m)
             tot = jnp.sum(w, axis=0, keepdims=True)
             acc = lax.dot_general(
-                v_ref[...], w.astype(jnp.bfloat16), TN, preferred_element_type=jnp.float32
+                keys_of(v_ref, values_ref), w.astype(jnp.bfloat16), TN, preferred_element_type=jnp.float32
             ).astype(o_ref.dtype)
             for inner in range(0, tile, lanes):
                 t = (start + inner) // lanes
@@ -69,6 +83,9 @@
     @pl.when((own // split == step) & (own % split == 0))
     def _():
         tree = tk_ref.shape[0]
+        if scratch:
+            tree_keys_ref[...] = jnp.swapaxes(tk_ref[...], 0, 1)
+            tree_values_ref[...] = jnp.swapaxes(tv_ref[...], 0, 1)
 
         def reach(parent_row):
             width = parent_row.shape[1]
@@ -77,19 +94,19 @@
             hit = (parent_row == key) | (token == key)
             return jnp.where(hit, 1.0, 0.0)
 
-        wide = reach(parents_ref[0:1, :])
+        wide = reach(jnp.concatenate([parents_ref[pl.ds(request, 1), :]] * (columns // tree), axis=1))
         square = wide[:, :tree]
         for _ in range(max(1, (tree - 1).bit_length())):
             left = square.astype(jnp.bfloat16)
             wide = jnp.minimum(jnp.dot(left, wide.astype(jnp.bfloat16), preferred_element_type=jnp.float32), 1.0)
             square = wide[:, :tree]
-        s = lax.dot_general(tk_ref[...], q_ref[...], NT, preferred_element_type=jnp.float32)
+        s = lax.dot_general(keys_of(tk_ref, tree_keys_ref), q_ref[...], NT, preferred_element_type=jnp.float32)
         allowed = wide > 0.5
         s = jnp.where(allowed, s * score_scale, lowest)
         m = jnp.max(s, axis=0, keepdims=True)
         w = jnp.where(allowed, jnp.exp2(s - m), 0.0)
         tot = jnp.sum(w, axis=0, keepdims=True)
-        acc = lax.dot_general(tv_ref[...], w.astype(jnp.bfloat16), TN, preferred_element_type=jnp.float32)
+        acc = lax.dot_general(keys_of(tv_ref, tree_values_ref), w.astype(jnp.bfloat16), TN, preferred_element_type=jnp.float32)
         for t in range(streams):
             here = slice(t * lanes, (t + 1) * lanes)
             m_old = ml_ref[t, 0:1, :]
@@ -321,7 +338,17 @@
 
     q = queries.reshape(requests, tree, kv_heads, group, head_size).transpose(0, 2, 3, 1, 4)
     q = q.reshape(pairs, columns, head_size)
-    parent_rows = jnp.broadcast_to(jnp.tile(parents, (1, group))[:, None, :], (requests, 8, columns))
+
+    inside = kv_heads % 4 == 0
+    if not inside:
+        cache_keys, cache_values, new_keys, new_values = map(by_head, (cache_keys, cache_values, new_keys, new_values))
+    split_scratch = [pltpu.VMEM((kv_heads, rows, head_size), jnp.bfloat16)
+                     for rows in (block_size, block_size, tree, tree) if inside]
+
+    def key_block(rows):
+        if inside:
+            return pl.BlockSpec((None, rows, kv_heads, head_size), lambda p, *_: (p // kv_heads, 0, 0, 0))
+        return pair_block(rows)
 
     def pair_block(rows):
         return pl.BlockSpec((None, rows, head_size), lambda p, *_: (p, 0, 0))
@@ -332,22 +359,22 @@
             num_scalar_prefetch=2,
             grid=(pairs,),
             in_specs=[
-                pair_block(columns), pair_block(block_size), pair_block(block_size),
-                pair_block(tree), pair_block(tree),
-                pl.BlockSpec((None, 8, columns), lambda p, *_: (p // kv_heads, 0, 0)),
+                pair_block(columns), key_block(block_size), key_block(block_size),
+                key_block(tree), key_block(tree),
+                pl.BlockSpec(parents.shape, lambda p, *_: (0, 0)),
             ],
             out_specs=[
                 pl.BlockSpec((streams, None, head_size, lanes), lambda p, *_: (0, p, 0, 0)),
                 pl.BlockSpec((streams, None, 2, lanes), lambda p, *_: (0, p, 0, 0)),
             ],
+            scratch_shapes=split_scratch,
         ),
         out_shape=[
             jax.ShapeDtypeStruct((streams, pairs, head_size, lanes), jnp.bfloat16),
             jax.ShapeDtypeStruct((streams, pairs, 2, lanes), jnp.float32),
         ],
         compiler_params=pltpu.CompilerParams(vmem_limit_bytes=48 * 1024 * 1024),
-    )(kv_lengths, me[None].astype(jnp.int32), q, by_head(cache_keys), by_head(cache_values),
-      by_head(new_keys), by_head(new_values), parent_rows)
+    )(kv_lengths, me[None].astype(jnp.int32), q, cache_keys, cache_values, new_keys, new_values, parents)
 
     fused = (requests, tree) if n == pairs and lanes == head_size else None
     o = o.reshape(streams, n, deep, lanes)

time: 121 us -> 103 us (0.85)
  local copies, waits for them, and re-layouts: 22.3 us -> 3.13 us
    transpose x4 -> x0, local copies, waits for them, and re-layouts: 18.5 us -> none  [by_head(): return array.transpose(0, 2, 1, 3).reshape(pairs, array.shape[1], head_size)]
where the time goes in v3:
time: 103 us
  Pallas kernels  99.3 us (96%)
  local copies, waits for them, and re-layouts  3.13 us (3%)
    pallas_call x1, Pallas kernels, body(): pl.pallas_call(functools.partial(attend_kernel, kv_heads, split, stages,...  49.9 us
    pallas_call x1, Pallas kernels, body(): pl.pallas_call(functools.partial(merge_kernel, n, stages, split, orders,...  49.4 us
    reshape x1, local copies, waits for them, and re-layouts, body(): queries.reshape(requests, tree, kv_heads, group, head_size)  2.46 us

profile of v3, /device:TPU:0, one launch (start us, length us, event | category | flops | bytes accessed | tf_op | source)
XLA Modules:
  0.0 102.5 jit_solution(15696514854918627100)
XLA Ops:
  0.0 0.0 copy-start.3
  0.0 0.0 copy-start.2
  0.0 0.0 copy-start.1
  0.0 0.0 copy-start
  0.0 2.5 %copy.9 = bf16[4,64,4,8,128]{4,1,3,2,0:T(8,128)(2,1)S(1)} copy(bf16[4,64,4,8,128]{4,3,2,1,0:T(8,128)(2,1)} %bitcast.6) | data formatting | bytes 4194304 | tf_op jit(solution)/shard_map/reshape | solution.py:339
  2.5 0.0 copy-done.3
  2.5 0.0 copy-done.2
  2.5 0.0 copy-done.1
  2.5 0.0 copy-done
  2.5 49.9 %shard_map.82 = (bf16[4,16,128,128]{3,2,1,0:T(8,128)(2,1)S(1)}, f32[4,16,2,128]{3,2,1,0:T(2,128)S(1)}) custom-call(s32[4]{0:T(128)S(1)} %copy-done.3, s32[1]{0:T(128)} %bitcast.place_ref, bf16[16,512,128]{2,1,0:T(8,128)(2,1)S(1)} %bitcast.5, bf16[4,2048,4,128]{3,2,1,0:T(4,128)(2,1)} %k_ref.1, bf16[4,2048,4,128]{3,2,1,0:T(4,128)(2,1)} %v_ref.1, ...), custom_call_target="tpu_custom_call" | custom-call | tf_op jit(solution)/shard_map/pallas_call | solution.py:356
  52.4 49.4 %shard_map.83 = bf16[128,512]{1,0:T(8,128)(2,1)S(1)} custom-call(bf16[4,16,128,128]{3,2,1,0:T(8,128)(2,1)S(1)} %get-tuple-element.7.o_ref, f32[4,16,2,128]{3,2,1,0:T(2,128)S(1)} %get-tuple-element.8.ml_ref, bf16[4096,512]{1,0:T(8,128)(2,1)} %refs_0_.1), custom_call_target="tpu_custom_call" | custom-call | tf_op jit(solution)/shard_map/pallas_call | solution.py:401
  101.9 0.7 copy.11
Async XLA Ops:
  0.0 2.5 %copy-start.3 = (s32[4]{0:T(128)S(1)}, s32[4]{0:T(128)}, u32[]{:S(2)}) copy-start(s32[4]{0:T(128)} %lengths_ref.1) | copy-start | bytes 52
  0.0 2.5 %copy-start.2 = (s32[4,64]{1,0:T(4,128)S(1)}, s32[4,64]{1,0:T(4,128)}, u32[]{:S(2)}) copy-start(s32[4,64]{1,0:T(4,128)} %parents_ref.1) | copy-start | bytes 3076
  0.0 2.5 %copy-start.1 = (bf16[4,64,4,128]{3,2,1,0:T(4,128)(2,1)S(1)}, bf16[4,64,4,128]{3,2,1,0:T(4,128)(2,1)}, u32[]{:S(2)}) copy-start(bf16[4,64,4,128]{3,2,1,0:T(4,128)(2,1)} %tv_ref.1) | copy-start | bytes 786436
  0.0 2.5 %copy-start = (bf16[4,64,4,128]{3,2,1,0:T(4,128)(2,1)S(1)}, bf16[4,64,4,128]{3,2,1,0:T(4,128)(2,1)}, u32[]{:S(2)}) copy-start(bf16[4,64,4,128]{3,2,1,0:T(4,128)(2,1)} %tk_ref.1) | copy-start | bytes 786436

commit v4 on v3

--- a/solution.py
+++ b/solution.py
@@ -20,35 +20,50 @@
     return result
 
 
+def split_heads(source, target):
+    rows, kv_heads, head_size = source.shape
+    flat = source[...].reshape(rows, kv_heads * head_size)
+    for h in range(kv_heads):
+        target[h] = flat[:, h * head_size:(h + 1) * head_size]
+
+
 def attend_kernel(kv_heads, split, stages, score_scale, lengths_ref, place_ref, q_ref, k_ref, v_ref,
                   tk_ref, tv_ref, parents_ref, o_ref, ml_ref, *scratch):
     step = pl.program_id(0)
     block_size = k_ref.shape[0]
     head = step % kv_heads
-    columns = q_ref.shape[0]
-    tile = columns
     streams, _, lanes = o_ref.shape
+    columns = streams * lanes
     request = step // kv_heads
     me = place_ref[0]
     valid = lengths_ref[request] - me * block_size
     if scratch:
-        keys_ref, values_ref, tree_keys_ref, tree_values_ref = scratch
+        keys_ref, values_ref, tree_keys_ref, tree_values_ref, queries_ref = scratch
 
         @pl.when((head == 0) & (valid > 0))
         def _():
-            keys_ref[...] = jnp.swapaxes(k_ref[...], 0, 1)
-            values_ref[...] = jnp.swapaxes(v_ref[...], 0, 1)
+            split_heads(k_ref, keys_ref)
+            split_heads(v_ref, values_ref)
+
+        @pl.when(head == 0)
+        def _():
+            tokens, heads, head_size = q_ref.shape
+            flat = q_ref[...].reshape(tokens, heads * head_size)
+            group = heads // kv_heads
+            for h in range(heads):
+                queries_ref[h // group, (h % group) * tokens:(h % group + 1) * tokens, :] = (
+                    flat[:, h * head_size:(h + 1) * head_size])
 
     def keys_of(ref, split_ref):
         return split_ref[head] if scratch else ref[...]
 
     if not scratch:
-        keys_ref = values_ref = tree_keys_ref = tree_values_ref = None
+        keys_ref = values_ref = tree_keys_ref = tree_values_ref = queries_ref = None
 
     def write(masked):
-        for start in range(0, columns, tile):
-            here = pl.ds(start, tile)
-            s = lax.dot_general(keys_of(k_ref, keys_ref), q_ref[here, :], NT, preferred_element_type=jnp.float32)
+        for start in (0,):
+            tile = columns
+            s = lax.dot_general(keys_of(k_ref, keys_ref), keys_of(q_ref, queries_ref), NT, preferred_element_type=jnp.float32)
             if masked:
                 rows = lax.broadcasted_iota(jnp.int32, s.shape, 0)
                 s = jnp.where(rows < valid, s, lowest)
@@ -100,7 +115,7 @@
             left = square.astype(jnp.bfloat16)
             wide = jnp.minimum(jnp.dot(left, wide.astype(jnp.bfloat16), preferred_element_type=jnp.float32), 1.0)
             square = wide[:, :tree]
-        s = lax.dot_general(keys_of(tk_ref, tree_keys_ref), q_ref[...], NT, preferred_element_type=jnp.float32)
+        s = lax.dot_general(keys_of(tk_ref, tree_keys_ref), keys_of(q_ref, queries_ref), NT, preferred_element_type=jnp.float32)
         allowed = wide > 0.5
         s = jnp.where(allowed, s * score_scale, lowest)
         m = jnp.max(s, axis=0, keepdims=True)
@@ -336,14 +351,15 @@
     def by_head(array):
         return array.transpose(0, 2, 1, 3).reshape(pairs, array.shape[1], head_size)
 
-    q = queries.reshape(requests, tree, kv_heads, group, head_size).transpose(0, 2, 3, 1, 4)
-    q = q.reshape(pairs, columns, head_size)
+    q = queries
 
     inside = kv_heads % 4 == 0
     if not inside:
+        q = queries.reshape(requests, tree, kv_heads, group, head_size).transpose(0, 2, 3, 1, 4)
+        q = q.reshape(pairs, columns, head_size)
         cache_keys, cache_values, new_keys, new_values = map(by_head, (cache_keys, cache_values, new_keys, new_values))
     split_scratch = [pltpu.VMEM((kv_heads, rows, head_size), jnp.bfloat16)
-                     for rows in (block_size, block_size, tree, tree) if inside]
+                     for rows in (block_size, block_size, tree, tree, columns) if inside]
 
     def key_block(rows):
         if inside:
@@ -352,6 +368,10 @@
 
     def pair_block(rows):
         return pl.BlockSpec((None, rows, head_size), lambda p, *_: (p, 0, 0))
+
+    query_block = pair_block(columns)
+    if inside:
+        query_block = pl.BlockSpec((None,) + queries.shape[1:], lambda p, *_: (p // kv_heads, 0, 0, 0))
 
     o, ml = pl.pallas_call(
         functools.partial(attend_kernel, kv_heads, split, stages, score_scale),
@@ -359,7 +379,7 @@
             num_scalar_prefetch=2,
             grid=(pairs,),
             in_specs=[
-                pair_block(columns), key_block(block_size), key_block(block_size),
+                query_block, key_block(block_size), key_block(block_size),
                 key_block(tree), key_block(tree),
                 pl.BlockSpec(parents.shape, lambda p, *_: (0, 0)),
             ],

time: 103 us -> 96.4 us (0.936)
  Pallas kernels: 99.3 us -> 90.6 us
  local copies, waits for them, and re-layouts: 3.13 us -> 5.48 us
    pallas_call x1, Pallas kernels: 49.9 us -> 41.2 us  [body(): pl.pallas_call(functools.partial(attend_kernel, kv_heads, split, stages,...]
    unnamed x9 -> x11, local copies, waits for them, and re-layouts: 0.67 us -> 5.48 us
    reshape x1 -> x0, local copies, waits for them, and re-layouts: 2.46 us -> none  [body(): queries.reshape(requests, tree, kv_heads, group, head_size)]
where the time goes in v4:
time: 96.4 us; the launch traced here: 96.1 us
  Pallas kernels  90.6 us (94%)
  local copies, waits for them, and re-layouts  5.48 us (6%)
    pallas_call x1, Pallas kernels, body(): pl.pallas_call(functools.partial(merge_kernel, n, stages, split, orders,...  49.5 us
    pallas_call x1, Pallas kernels, body(): pl.pallas_call(functools.partial(attend_kernel, kv_heads, split, stages,...  41.2 us
    unnamed x11, local copies, waits for them, and re-layouts  5.48 us

profile of v4, /device:TPU:0, one launch (start us, length us, event | category | flops | bytes accessed | tf_op | source)
XLA Modules:
  0.0 96.1 jit_solution(9567965236778036882)
XLA Ops:
  0.0 0.0 copy-start
  0.0 1.6 %copy-done = bf16[4,64,32,128]{3,2,1,0:T(8,128)(2,1)S(1)} copy-done((bf16[4,64,32,128]{3,2,1,0:T(8,128)(2,1)S(1)}, bf16[4,64,32,128]{3,2,1,0:T(8,128)(2,1)}, u32[]{:S(2)}) %copy-start) | copy-done | bytes 2097176
  1.6 0.0 copy-start.1
  1.6 0.9 copy-done.1
  2.5 0.0 copy-start.2
  2.5 0.9 copy-done.2
  3.5 0.0 copy-start.3
  3.5 0.7 copy-done.3
  4.2 0.0 copy-start.4
  4.2 0.7 copy-done.4
  4.8 41.2 %shard_map.82 = (bf16[4,16,128,128]{3,2,1,0:T(8,128)(2,1)S(1)}, f32[4,16,2,128]{3,2,1,0:T(2,128)S(1)}) custom-call(s32[4]{0:T(128)S(1)} %copy-done.4, s32[1]{0:T(128)} %bitcast.place_ref, bf16[4,64,32,128]{3,2,1,0:T(8,128)(2,1)S(1)} %copy-done, bf16[4,2048,4,128]{3,2,1,0:T(4,128)(2,1)} %k_ref.1, bf16[4,2048,4,128]{3,2,1,0:T(4,128)(2,1)} %v_ref.1, ...), custom_call_target="tpu_custom_call" | custom-call | tf_op jit(solution)/shard_map/pallas_call | solution.py:376
  46.0 49.5 %shard_map.83 = bf16[128,512]{1,0:T(8,128)(2,1)S(1)} custom-call(bf16[4,16,128,128]{3,2,1,0:T(8,128)(2,1)S(1)} %get-tuple-element.7.o_ref, f32[4,16,2,128]{3,2,1,0:T(2,128)S(1)} %get-tuple-element.8.ml_ref, bf16[4096,512]{1,0:T(8,128)(2,1)} %refs_0_.1), custom_call_target="tpu_custom_call" | custom-call | tf_op jit(solution)/shard_map/pallas_call | solution.py:421
  95.5 0.7 copy.10
Async XLA Ops:
  0.0 1.6 %copy-start = (bf16[4,64,32,128]{3,2,1,0:T(8,128)(2,1)S(1)}, bf16[4,64,32,128]{3,2,1,0:T(8,128)(2,1)}, u32[]{:S(2)}) copy-start(bf16[4,64,32,128]{3,2,1,0:T(8,128)(2,1)} %q_ref.1) | copy-start | bytes 6291460
  1.6 0.9 copy-start.1
  2.5 0.9 copy-start.2
  3.5 0.7 copy-start.3
  4.2 0.7 copy-start.4
